TPU v7x, 256 devices: a whole 4x4x8 slice. The times are simulated.
256 devices in a mesh: leaf: 32 (over z, y), front: 8 (over x, core).
Axes of the slice: x: 4, y: 4, z: 8, core: 2. Of those that a mesh axis runs over, the one named last changes fastest.
Arguments:
- section_updates: bfloat16 [32768, 256], P(('leaf', 'front')), may hold values from -6 to 6
- upper_rhs: float32 [126976, 256], P(('leaf', 'front')), may hold values from -6 to 6
- pivot_inverse: bfloat16 [126976, 4096], P('leaf', 'front'), may hold values from -0.09375 to 0.09375
- coupling: bfloat16 [1024, 122880], P('front', 'leaf'), may hold values from -0.09375 to 0.09375
- extend_lists: int32 [62, 8], replicated, may hold values from 0 to 39, as said below
Outputs:
- solution: float32 [126976, 256], P(('leaf', 'front'))
- interface: bfloat16 [32768, 256], P(('leaf', 'front'))
Inputs may be any that keep to these rules, and one draw needn't show every extreme that they name: `extend_lists`: each row names 8 different blocks of the parent's frame; the rows of the root's two children name pivot blocks only, below 32.
All inputs are finite; a program needn't handle non-finite values.
Results may differ from a plain program's by a relative error of at most 0.022.
Values may be sent and summed in bfloat16 or wider, within the bound.
A program may use at most 64 MiB of HBM per device.

v0:
```python
import jax
import jax.numpy as jnp
from jax import lax
from jax.sharding import PartitionSpec as P

PIV = 4096
UPD = 1024
BLK = 128


def partner(block, axis, stride):
    count = lax.axis_size(axis)
    route = []
    for low in range(count):
        high = low | 1 << stride
        if high != low and high < count:
            route += [(low, high), (high, low)]
    return lax.ppermute(block, axis, route)


def child_base(leaves, height):
    total_rows = 0
    for depth in range(height - 1):
        total_rows = total_rows + leaves // 2**depth
    return total_rows


def list_row(extend_lists, row_index):
    return lax.dynamic_slice_in_dim(extend_lists, row_index, 1, 0)[0]


def upper_bit(position, bit_index):
    return position >> bit_index & 1 == 1


def joined(position, bit_index, portion, partner_rows):
    return jnp.where(
        upper_bit(position, bit_index),
        jnp.concatenate([partner_rows, portion], 0),
        jnp.concatenate([portion, partner_rows], 0),
    )


def gather_own(portion, height, position):
    for bit_index in range(height):
        partner_rows = partner(portion.astype(jnp.bfloat16), "leaf", bit_index).astype(
            portion.dtype
        )
        portion = joined(position, bit_index, portion, partner_rows)
    return portion


def sum_updates(summand, height):
    for bit_index in range(height):
        summand = summand + partner(summand.astype(jnp.bfloat16), "leaf", bit_index).astype(
            summand.dtype
        )
    return summand


def sum_solution(summand, height):
    for bit_index in range(height):
        summand = summand + partner(summand.astype(jnp.bfloat16), "leaf", bit_index).astype(
            summand.dtype
        )
    return summand


def per_device(section_updates, upper_rhs, pivot_inverse, coupling, extend_lists):
    leaves = lax.axis_size("leaf")
    fronts = lax.axis_size("front")
    levels = leaves.bit_length() - 1
    position = lax.axis_index("leaf")
    column = lax.axis_index("front")
    rhs_width = upper_rhs.shape[1]
    piv_dev = PIV // fronts
    upd_dev = UPD // fronts
    piv_blocks = piv_dev // BLK
    upd_blocks = upd_dev // BLK
    block_count = UPD // BLK
    local_blocks = jnp.concatenate(
        [
            column * piv_blocks + jnp.arange(piv_blocks, dtype=jnp.int32),
            PIV // BLK + column * upd_blocks + jnp.arange(upd_blocks, dtype=jnp.int32),
        ]
    )
    local_count = piv_blocks + upd_blocks
    carried = section_updates
    saved_part = []
    saved_half = []
    for height in range(1, levels + 1):
        group_size = 2**height
        span_rows = PIV // group_size
        band_start = PIV - PIV // 2 ** (height - 1)
        rhs_len = piv_dev // group_size
        rhs_start = piv_dev - piv_dev // 2 ** (height - 1)
        member = position & group_size - 1
        own_child = child_base(leaves, height) + (position >> height - 1)
        sibling = partner(carried, "leaf", height - 1)
        pair_blocks = lax.all_gather(jnp.stack([carried, sibling]), "front", axis=1, tiled=True)
        pair_lists = jnp.stack(
            [list_row(extend_lists, own_child), list_row(extend_lists, own_child ^ 1)]
        )
        chooser = (pair_lists.reshape(2 * block_count)[None, :] == local_blocks[:, None]).astype(
            jnp.bfloat16
        )
        assembled = jnp.dot(
            chooser,
            pair_blocks.reshape(2 * block_count, BLK * rhs_width),
            preferred_element_type=jnp.float32,
        ).reshape(local_count * BLK, rhs_width)
        own_rows = gather_own(upper_rhs[rhs_start : rhs_start + rhs_len], height, position)
        rows_half = (own_rows + assembled[:piv_dev]).astype(jnp.bfloat16)
        g_share = pivot_inverse[band_start : band_start + span_rows]
        pivot_part = lax.psum(
            jnp.dot(g_share, rows_half, preferred_element_type=jnp.float32).astype(jnp.bfloat16),
            "front",
        ).astype(jnp.float32)
        pivot_half = pivot_part.astype(jnp.bfloat16)
        saved_part.append(pivot_part)
        saved_half.append(pivot_half)
        if height < levels:
            c_share = coupling[:, band_start : band_start + span_rows]
            summand = jnp.dot(c_share, pivot_half, preferred_element_type=jnp.float32)
            frame_upd = assembled[piv_dev:]
            carried = (frame_upd - sum_updates(summand, height)).astype(jnp.bfloat16)
    from_above = carried
    outputs = []
    for height in range(levels, 0, -1):
        group_size = 2**height
        span_rows = PIV // group_size
        band_start = PIV - PIV // 2 ** (height - 1)
        member = position & group_size - 1
        pivot_part = saved_part[height - 1]
        if height < levels:
            c_share = coupling[:, band_start : band_start + span_rows]
            back_total = lax.psum(
                jnp.einsum(
                    "up,ur->pr", c_share, from_above, preferred_element_type=jnp.float32
                ).astype(jnp.bfloat16),
                "front",
            ).astype(jnp.float32)
            weight_half = (pivot_part - back_total).astype(jnp.bfloat16)
            upper_rows = from_above
        else:
            weight_half = saved_half[height - 1]
            upper_rows = jnp.zeros((upd_dev, rhs_width), jnp.bfloat16)
        g_share = pivot_inverse[band_start : band_start + span_rows]
        solve_term = jnp.einsum(
            "cp,cr->pr", g_share, weight_half, preferred_element_type=jnp.float32
        )
        part_len = piv_dev // group_size
        summed = sum_solution(solve_term, height)
        portion = lax.dynamic_slice_in_dim(summed, member * part_len, part_len, 0)
        rows_half = summed.astype(jnp.bfloat16)
        outputs.append(portion)
        frame_half = jnp.concatenate([rows_half, upper_rows], 0).reshape(
            local_count, BLK * rhs_width
        )
        child_list = list_row(extend_lists, child_base(leaves, height) + (position >> height - 1))
        picker = (child_list[:, None] == local_blocks[None, :]).astype(jnp.bfloat16)
        outgoing = (
            jnp.dot(picker, frame_half, preferred_element_type=jnp.float32)
            .astype(jnp.bfloat16)
            .reshape(fronts, upd_dev, rhs_width)
        )
        incoming = lax.all_to_all(outgoing, "front", split_axis=0, concat_axis=0, tiled=True)
        from_above = jnp.sum(incoming, axis=0, dtype=jnp.float32).astype(jnp.bfloat16)
    solution = jnp.concatenate(outputs[::-1], 0)
    return (solution, from_above)


def solution(mesh):
    placed = (
        P(("leaf", "front"), None),
        P(("leaf", "front"), None),
        P("leaf", "front"),
        P("front", "leaf"),
        P(),
    )
    return jax.shard_map(
        per_device,
        mesh=mesh,
        in_specs=placed,
        out_specs=(P(("leaf", "front"), None), P(("leaf", "front"), None)),
        check_vma=False,
    )
```

profile of v0, /device:TPU:1, one launch (start us, length us, event | category | flops | bytes accessed | tf_op | source)
XLA Modules:
  0.0 1092.0 jit_solution(5823587160174523353)
XLA Ops:
  18.5 25.0 %all-gather.6.cloned.1.call-done = bf16[2,1024,256]{2,1,0:T(8,128)(2,1)} async-done(((bf16[2,128,256]{2,1,0:T(8,128)(2,1)}), bf16[2,1024,256]{2,1,0:T(8,128)(2,1)}) %all-gather.6.cloned.1.call-update) | async-done | bytes 1048592 | tf_op jit(solution)/shard_map/all_gather | solution.py:100
  45.9 3.6 fusion
  49.5 65.4 %all-reduce.11.cloned.1.call-done = bf16[2048,256]{0,1:T(8,128)(2,1)} async-done(((bf16[2048,256]{0,1:T(8,128)(2,1)}), bf16[2048,256]{0,1:T(8,128)(2,1)}) %all-reduce.11.cloned.1.call-update) | async-done | bytes 1048592 | tf_op jit(solution)/shard_map/psum | solution.py:115
  119.8 2.8 collective-permute-start.5
  126.6 2.5 collective-permute-done.2
  129.8 2.5 collective-permute-start.3
  132.5 2.6 collective-permute-done.3
  135.2 20.1 %all-gather.8.cloned.1.call-done = bf16[2,1024,256]{1,2,0:T(8,128)(2,1)} async-done(((bf16[2,128,256]{1,2,0:T(8,128)(2,1)}), bf16[2,1024,256]{1,2,0:T(8,128)(2,1)}) %all-gather.8.cloned.1.call-update) | async-done | bytes 1048592 | tf_op jit(solution)/shard_map/all_gather | solution.py:100
  158.9 2.8 fusion.6
  161.8 64.7 %all-reduce.13.cloned.1.call-done = bf16[1024,256]{0,1:T(8,128)(2,1)} async-done(((bf16[1024,256]{0,1:T(8,128)(2,1)}), bf16[1024,256]{0,1:T(8,128)(2,1)}) %all-reduce.13.cloned.1.call-update) | async-done | bytes 524304 | tf_op jit(solution)/shard_map/psum | solution.py:115
  231.1 2.8 collective-permute-start.10
  242.7 3.3 collective-permute-start.7
  252.5 18.5 %all-gather.10.cloned.1.call-done = bf16[2,1024,256]{1,2,0:T(8,128)(2,1)} async-done(((bf16[2,128,256]{1,2,0:T(8,128)(2,1)}), bf16[2,1024,256]{1,2,0:T(8,128)(2,1)}) %all-gather.10.cloned.1.call-update) | async-done | bytes 1048592 | tf_op jit(solution)/shard_map/all_gather | solution.py:100
  274.6 2.4 fusion.10
  277.1 63.9 %all-reduce.15.cloned.1.call-done = bf16[512,256]{0,1:T(8,128)(2,1)} async-done(((bf16[512,256]{0,1:T(8,128)(2,1)}), bf16[512,256]{0,1:T(8,128)(2,1)}) %all-reduce.15.cloned.1.call-update) | async-done | bytes 262160 | tf_op jit(solution)/shard_map/psum | solution.py:115
  345.4 2.8 collective-permute-start.17
  353.4 2.3 collective-permute-start.19
  361.0 2.8 collective-permute-start.13
  369.3 2.9 collective-permute-start.15
  372.3 3.6 collective-permute-done.15
  376.0 15.2 %all-gather.12.cloned.1.call-done = bf16[2,1024,256]{1,2,0:T(8,128)(2,1)} async-done(((bf16[2,128,256]{1,2,0:T(8,128)(2,1)}), bf16[2,1024,256]{1,2,0:T(8,128)(2,1)}) %all-gather.12.cloned.1.call-update) | async-done | bytes 1048592 | tf_op jit(solution)/shard_map/all_gather | solution.py:100
  397.1 63.6 %all-reduce.17.cloned.1.call-done = bf16[256,256]{0,1:T(8,128)(2,1)} async-done(((bf16[256,256]{0,1:T(8,128)(2,1)}), bf16[256,256]{0,1:T(8,128)(2,1)}) %all-reduce.17.cloned.1.call-update) | async-done | bytes 131088 | tf_op jit(solution)/shard_map/psum | solution.py:115
  465.0 2.7 collective-permute-start.26
  477.2 6.3 collective-permute-start.29
  488.6 2.8 collective-permute-start.21
  493.4 2.5 collective-permute-done.22
  498.3 2.5 collective-permute-done.23
  501.5 5.0 collective-permute-start.24
  506.6 2.7 collective-permute-done.24
  509.4 11.0 %all-gather.14.cloned.1.call-done = bf16[2,1024,256]{1,2,0:T(8,128)(2,1)} async-done(((bf16[2,128,256]{1,2,0:T(8,128)(2,1)}), bf16[2,1024,256]{1,2,0:T(8,128)(2,1)}) %all-gather.14.cloned.1.call-update) | async-done | bytes 1048592 | tf_op jit(solution)/shard_map/all_gather | solution.py:100
  525.2 66.1 %all-reduce.19.cloned.1.call-done = bf16[128,256]{0,1:T(8,128)(2,1)} async-done(((bf16[128,256]{0,1:T(8,128)(2,1)}), bf16[128,256]{0,1:T(8,128)(2,1)}) %all-reduce.19.cloned.1.call-update) | async-done | bytes 65552 | tf_op jit(solution)/shard_map/psum | solution.py:115
  593.5 4.2 collective-permute-done.30
  597.8 2.6 collective-permute-start.31
  600.4 5.5 collective-permute-done.31
  607.4 4.0 collective-permute-done.32
  611.5 2.3 collective-permute-start.33
  613.8 6.7 collective-permute-done.33
  620.6 5.5 collective-permute-start.34
  626.2 6.8 collective-permute-done.34
  634.9 30.3 %all_to_all.25 = bf16[8,128,256]{2,1,0:T(8,128)(2,1)S(1)} all-to-all(bf16[8,128,256]{2,1,0:T(8,128)(2,1)S(1)} %copy.50), channel_id=1, replica_groups=mesh['leaf'=32,'front'=8] {'front'}, dimensions={0} | all-to-all | bytes 1048576 | tf_op jit(solution)/shard_map/all_to_all | solution.py:167
  666.2 59.3 %all-reduce.21.cloned.1.call-done = bf16[256,256]{0,1:T(8,128)(2,1)} async-done(((bf16[256,256]{0,1:T(8,128)(2,1)}), bf16[256,256]{0,1:T(8,128)(2,1)}) %all-reduce.21.cloned.1.call-update) | async-done | bytes 131088 | tf_op jit(solution)/shard_map/psum | solution.py:137
  728.0 4.1 collective-permute-done.35
  732.2 2.7 collective-permute-start.36
  734.9 5.4 collective-permute-done.36
  741.8 3.9 collective-permute-done.37
  745.9 2.6 collective-permute-start.38
  748.6 6.6 collective-permute-done.38
  757.2 24.9 %all_to_all.26 = bf16[8,128,256]{2,1,0:T(8,128)(2,1)S(1)} all-to-all(bf16[8,128,256]{2,1,0:T(8,128)(2,1)S(1)} %copy.54), channel_id=1, replica_groups=mesh['leaf'=32,'front'=8] {'front'}, dimensions={0} | all-to-all | bytes 1048576 | tf_op jit(solution)/shard_map/all_to_all | solution.py:167
  783.2 62.7 %all-reduce.23.cloned.1.call-done = bf16[512,256]{0,1:T(8,128)(2,1)} async-done(((bf16[512,256]{0,1:T(8,128)(2,1)}), bf16[512,256]{0,1:T(8,128)(2,1)}) %all-reduce.23.cloned.1.call-update) | async-done | bytes 262160 | tf_op jit(solution)/shard_map/psum | solution.py:137
  848.6 4.1 collective-permute-done.39
  852.7 2.8 collective-permute-start.40
  855.5 5.4 collective-permute-done.40
  862.5 3.8 collective-permute-done.41
  868.3 20.9 %all_to_all.27 = bf16[8,128,256]{2,1,0:T(8,128)(2,1)S(1)} all-to-all(bf16[8,128,256]{2,1,0:T(8,128)(2,1)S(1)} %copy.58), channel_id=1, replica_groups=mesh['leaf'=32,'front'=8] {'front'}, dimensions={0} | all-to-all | bytes 1048576 | tf_op jit(solution)/shard_map/all_to_all | solution.py:167
  890.4 63.8 %all-reduce.25.cloned.1.call-done = bf16[1024,256]{0,1:T(8,128)(2,1)} async-done(((bf16[1024,256]{0,1:T(8,128)(2,1)}), bf16[1024,256]{0,1:T(8,128)(2,1)}) %all-reduce.25.cloned.1.call-update) | async-done | bytes 524304 | tf_op jit(solution)/shard_map/psum | solution.py:137
  957.4 4.0 collective-permute-done.42
  961.5 2.8 collective-permute-start.43
  964.4 5.2 collective-permute-done.43
  970.8 19.0 %all_to_all.28 = bf16[8,128,256]{2,1,0:T(8,128)(2,1)S(1)} all-to-all(bf16[8,128,256]{2,1,0:T(8,128)(2,1)S(1)} %copy.62), channel_id=1, replica_groups=mesh['leaf'=32,'front'=8] {'front'}, dimensions={0} | all-to-all | bytes 1048576 | tf_op jit(solution)/shard_map/all_to_all | solution.py:167
  991.3 65.7 %all-reduce.27.cloned.1.call-done = bf16[2048,256]{0,1:T(8,128)(2,1)} async-done(((bf16[2048,256]{0,1:T(8,128)(2,1)}), bf16[2048,256]{0,1:T(8,128)(2,1)}) %all-reduce.27.cloned.1.call-update) | async-done | bytes 1048592 | tf_op jit(solution)/shard_map/psum | solution.py:137
  1057.0 2.6 fusion.133
  1062.0 2.9 collective-permute-done.44
  1066.9 8.3 all-to-all-start.4
  1078.4 6.1 all-to-all-done.4
  (275 shorter events, 141.5 us)
Async XLA Ops:
  7.2 36.2 %all-gather.6.cloned.1.call-start = ((), (), s32[]{:S(2)}) async-start(), calls=%async_computation.5 | async-start | bytes 1179648 | tf_op jit(solution)/shard_map/all_gather | solution.py:100
  7.2 4.1 collective-permute-start.1
  12.8 102.0 %all-reduce.11.cloned.1.call-start = ((), (), s32[]{:S(2)}) async-start(), calls=%async_computation.6 | async-start | bytes 2097152 | tf_op jit(solution)/shard_map/psum | solution.py:115
  13.8 3.9 collective-permute-start
  49.5 105.8 %all-gather.8.cloned.1.call-start = ((), (), s32[]{:S(2)}) async-start(), calls=%async_computation.7 | async-start | bytes 1179648 | tf_op jit(solution)/shard_map/all_gather | solution.py:100
  116.5 3.2 collective-permute-start.4
  119.8 4.8 collective-permute-start.5
  125.3 101.3 %all-reduce.13.cloned.1.call-start = ((), (), s32[]{:S(2)}) async-start(), calls=%async_computation.8 | async-start | bytes 1048576 | tf_op jit(solution)/shard_map/psum | solution.py:115
  125.3 3.7 collective-permute-start.2
  129.8 5.3 collective-permute-start.3
  161.7 109.2 %all-gather.10.cloned.1.call-start = ((), (), s32[]{:S(2)}) async-start(), calls=%async_computation.9 | async-start | bytes 1179648 | tf_op jit(solution)/shard_map/all_gather | solution.py:100
  227.9 3.2 collective-permute-start.9
  231.1 4.7 collective-permute-start.10
  235.8 3.2 collective-permute-start.11
  239.7 101.2 %all-reduce.15.cloned.1.call-start = ((), (), s32[]{:S(2)}) async-start(), calls=%async_computation.10 | async-start | bytes 524288 | tf_op jit(solution)/shard_map/psum | solution.py:115
  239.8 2.9 collective-permute-start.6
  242.7 5.2 collective-permute-start.7
  248.6 3.8 collective-permute-start.8
  277.0 114.2 %all-gather.12.cloned.1.call-start = ((), (), s32[]{:S(2)}) async-start(), calls=%async_computation.11 | async-start | bytes 1179648 | tf_op jit(solution)/shard_map/all_gather | solution.py:100
  342.2 3.2 collective-permute-start.16
  345.4 4.7 collective-permute-start.17
  350.1 3.2 collective-permute-start.18
  353.4 4.1 collective-permute-start.19
  358.2 102.5 %all-reduce.17.cloned.1.call-start = ((), (), s32[]{:S(2)}) async-start(), calls=%async_computation.12 | async-start | bytes 262144 | tf_op jit(solution)/shard_map/psum | solution.py:115
  358.3 2.7 collective-permute-start.12
  361.0 4.4 collective-permute-start.13
  365.3 3.2 collective-permute-start.14
  369.3 6.6 collective-permute-start.15
  393.2 92.8 %copy-start.6 = (f32[496,256]{1,0:T(8,128)S(1)}, f32[496,256]{1,0:T(8,128)}, u32[]{:S(2)}) copy-start(f32[496,256]{1,0:T(8,128)} %param.6) | copy-start | bytes 1523716
  394.5 94.0 %slice-start.4 = ((f32[496,256]{1,0:T(8,128)}), f32[16,256]{1,0:T(8,128)S(1)}, s32[]{:S(2)}) async-start(f32[496,256]{1,0:T(8,128)} %param.6), calls=%async_computation.23 | async-start | bytes 32768 | tf_op jit(solution)/shard_map/slice | solution.py:112
  397.1 123.3 %all-gather.14.cloned.1.call-start = ((), (), s32[]{:S(2)}) async-start(), calls=%async_computation.13 | async-start | bytes 1179648 | tf_op jit(solution)/shard_map/all_gather | solution.py:100
  461.8 3.2 collective-permute-start.25
  465.0 4.7 collective-permute-start.26
  469.8 3.2 collective-permute-start.27
  473.0 4.1 collective-permute-start.28
  477.2 8.1 collective-permute-start.29
  485.9 105.4 %all-reduce.19.cloned.1.call-start = ((), (), s32[]{:S(2)}) async-start(), calls=%async_computation.14 | async-start | bytes 131072 | tf_op jit(solution)/shard_map/psum | solution.py:115
  486.0 2.6 collective-permute-start.20
  488.6 4.5 collective-permute-start.21
  493.1 2.9 collective-permute-start.22
  496.0 4.8 collective-permute-start.23
  501.5 7.8 collective-permute-start.24
  525.1 200.5 %all-reduce.21.cloned.1.call-start = ((), (), s32[]{:S(2)}) async-start(), calls=%async_computation.15 | async-start | bytes 262144 | tf_op jit(solution)/shard_map/psum | solution.py:137
  592.4 5.3 collective-permute-start.30
  597.8 8.2 collective-permute-start.31
  606.1 5.3 collective-permute-start.32
  611.5 9.1 collective-permute-start.33
  620.6 104.9 %copy-start.9 = (bf16[256,256]{0,1:T(8,128)(2,1)S(1)}, bf16[256,256]{0,1:T(8,128)(2,1)}, u32[]{:S(2)}) copy-start(bf16[256,256]{0,1:T(8,128)(2,1)} %all-reduce.17.cloned.1.call-done) | copy-start | bytes 393220
  620.6 12.3 %collective-permute-start.34 = (bf16[512,256]{0,1:T(8,128)(2,1)S(1)}, bf16[512,256]{0,1:T(8,128)(2,1)S(1)}, u32[]{:S(2)}, u32[]{:S(2)}) collective-permute-start(bf16[512,256]{0,1:T(8,128)(2,1)S(1)} %fusion.51), channel_id=1, source_target_pairs={{0,128},{128,0},{8,136},{136,8},{16,144},{144,16},{24,152},{152,24... | collective-permute-start | bytes 786440 | tf_op jit(solution)/shard_map/ppermute | solution.py:18
  666.2 179.7 %all-reduce.23.cloned.1.call-start = ((), (), s32[]{:S(2)}) async-start(), calls=%async_computation.16 | async-start | bytes 524288 | tf_op jit(solution)/shard_map/psum | solution.py:137
  726.8 5.3 collective-permute-start.35
  732.2 8.2 collective-permute-start.36
  740.5 5.3 collective-permute-start.37
  745.9 9.3 collective-permute-start.38
  748.6 97.3 %copy-start.8 = (bf16[512,256]{0,1:T(8,128)(2,1)S(1)}, bf16[512,256]{0,1:T(8,128)(2,1)}, u32[]{:S(2)}) copy-start(bf16[512,256]{0,1:T(8,128)(2,1)} %all-reduce.15.cloned.1.call-done) | copy-start | bytes 786436
  783.1 171.1 %all-reduce.25.cloned.1.call-start = ((), (), s32[]{:S(2)}) async-start(), calls=%async_computation.17 | async-start | bytes 1048576 | tf_op jit(solution)/shard_map/psum | solution.py:137
  847.3 5.3 collective-permute-start.39
  852.7 8.2 collective-permute-start.40
  861.0 5.3 collective-permute-start.41
  890.4 166.6 %all-reduce.27.cloned.1.call-start = ((), (), s32[]{:S(2)}) async-start(), calls=%async_computation.18 | async-start | bytes 2097152 | tf_op jit(solution)/shard_map/psum | solution.py:137
  956.1 5.3 collective-permute-start.42
  961.5 8.2 collective-permute-start.43
  1059.6 5.3 collective-permute-start.44
  1066.9 17.6 %all-to-all-start.4 = ((bf16[8,128,256]{2,1,0:T(8,128)(2,1)}), bf16[8,128,256]{2,1,0:T(8,128)(2,1)S(1)}, u32[]{:S(2)}, u32[]{:S(2)}) async-start(bf16[8,128,256]{2,1,0:T(8,128)(2,1)} %copy.66), calls=%async_computation.4 | async-start | bytes 1048576 | tf_op jit(solution)/shard_map/all_to_all | solution.py:167
  (11 other events, 785.8 us)
Sparse Core Ops, SparseCore 0:
  12.9 30.4 all-gather.5
  49.6 65.2 all-reduce.10
  125.4 29.7 all-gather.7
  161.8 64.6 all-reduce.12
  239.9 31.0 all-gather.9
  277.1 63.8 all-reduce.14
  358.3 32.8 all-gather.11
  397.2 63.4 all-reduce.16
  486.0 34.3 all-gather.13
  525.2 66.0 all-reduce.18
  666.3 59.1 all-reduce.20
  783.3 62.6 all-reduce.22
  890.5 63.6 all-reduce.24
  991.4 65.4 all-reduce.26
where the time goes:
time: 1100 us; the launch traced here: 1090 us
  waiting for transfers between devices  799 us (73%)
  starting transfers between devices  105 us (10%)
  blocking collectives  95 us (9%)
  matrix products  34.2 us (3%)
  local copies, waits for them, and re-layouts  29.3 us (3%)
  between operations  15.1 us (1%)
  other arithmetic  13.8 us (1%)
    psum x5, waiting for transfers between devices, per_device(): lax.psum(jnp.dot(g_share, rows_half, preferred_element_type=jnp.float32)....  324 us
    psum x4, waiting for transfers between devices, per_device(): lax.psum(jnp.einsum('up,ur->pr', c_share, from_above, preferred_element_t...  252 us
    ppermute x45, waiting for transfers between devices, partner(): return lax.ppermute(block, axis, route)  128 us
    ppermute x45, starting transfers between devices, partner(): return lax.ppermute(block, axis, route)  96.3 us
    all_to_all x4, blocking collectives, per_device(): lax.all_to_all(outgoing, 'front', split_axis=0, concat_axis=0, tiled=True)  95 us
    all_gather x5, waiting for transfers between devices, per_device(): lax.all_gather(jnp.stack([carried, sibling]), 'front', axis=1, tiled=True)  89.7 us
  transfers between devices with their start and end apart: 60, of which 60 were waited for; matrix products, arithmetic and copies ran while one was open for 1% of the time, Pallas kernels for 0%

commit v1 on v0

--- a/solution.py
+++ b/solution.py
@@ -112,9 +112,14 @@
         own_rows = gather_own(upper_rhs[rhs_start : rhs_start + rhs_len], height, position)
         rows_half = (own_rows + assembled[:piv_dev]).astype(jnp.bfloat16)
         g_share = pivot_inverse[band_start : band_start + span_rows]
-        pivot_part = lax.psum(
-            jnp.dot(g_share, rows_half, preferred_element_type=jnp.float32).astype(jnp.bfloat16),
-            "front",
+        pivot_part = jnp.sum(
+            lax.all_gather(
+                jnp.dot(g_share, rows_half, preferred_element_type=jnp.float32).astype(
+                    jnp.bfloat16
+                ),
+                "front",
+            ),
+            axis=0,
         ).astype(jnp.float32)
         pivot_half = pivot_part.astype(jnp.bfloat16)
         saved_part.append(pivot_part)

time: 1100 us -> 996 us (0.905)
  waiting for transfers between devices: 799 us -> 625 us
  local copies, waits for them, and re-layouts: 29.3 us -> 73.7 us
  other arithmetic: 13.8 us -> 39.8 us
    psum x5 -> x0, waiting for transfers between devices: 324 us -> none  [per_device(): lax.psum(jnp.dot(g_share, rows_half, preferred_element_type=jnp.float32)....]
    all_gather x0 -> x4, waiting for transfers between devices: none -> 143 us  [per_device(): lax.all_gather(jnp.dot(g_share, rows_half, preferred_element_type=jnp.flo...]
    unnamed x22 -> x49, local copies, waits for them, and re-layouts: 2.15 us -> 31.1 us
    all_gather x0 -> x1, blocking collectives: none -> 18.3 us  [per_device(): lax.all_gather(jnp.dot(g_share, rows_half, preferred_element_type=jnp.flo...]
    reduce_sum x0 -> x5, other arithmetic: none -> 16.6 us  [per_device(): jnp.sum(lax.all_gather(jnp.dot(g_share, rows_half, preferred_element_type...]
    ppermute x45, waiting for transfers between devices: 128 us -> 144 us  [partner(): return lax.ppermute(block, axis, route)]
    all_to_all x4, blocking collectives: 95 us -> 79.5 us  [per_device(): lax.all_to_all(outgoing, 'front', split_axis=0, concat_axis=0, tiled=True)]
  transfers between devices with their start and end apart: 60 -> 59, of which waited for: 60 -> 57; matrix products, arithmetic and copies ran while one was open for 1% -> 2% of each run, Pallas kernels for 0% -> 0%
where the time goes in v1:
time: 996 us; the launch traced here: 992 us
  waiting for transfers between devices  625 us (63%)
  starting transfers between devices  104 us (10%)
  blocking collectives  97.8 us (10%)
  local copies, waits for them, and re-layouts  73.7 us (7%)
  other arithmetic  39.8 us (4%)
  matrix products  36 us (4%)
  between operations  15.1 us (2%)
    psum x4, waiting for transfers between devices, per_device(): lax.psum(jnp.einsum('up,ur->pr', c_share, from_above, preferred_element_t...  252 us
    ppermute x45, waiting for transfers between devices, partner(): return lax.ppermute(block, axis, route)  144 us
    all_gather x4, waiting for transfers between devices, per_device(): lax.all_gather(jnp.dot(g_share, rows_half, preferred_element_type=jnp.flo...  143 us
    ppermute x45, starting transfers between devices, partner(): return lax.ppermute(block, axis, route)  94 us
    all_gather x5, waiting for transfers between devices, per_device(): lax.all_gather(jnp.stack([carried, sibling]), 'front', axis=1, tiled=True)  81.7 us
    all_to_all x4, blocking collectives, per_device(): lax.all_to_all(outgoing, 'front', split_axis=0, concat_axis=0, tiled=True)  79.5 us
    unnamed x49, local copies, waits for them, and re-layouts  31.1 us
  transfers between devices with their start and end apart: 59, of which 57 were waited for; matrix products, arithmetic and copies ran while one was open for 2% of the time, Pallas kernels for 0%

profile of v1, /device:TPU:1, one launch (start us, length us, event | category | flops | bytes accessed | tf_op | source)
XLA Modules:
  0.0 991.6 jit_solution(3074532002690835983)
XLA Ops:
  15.4 2.5 fusion.112
  18.2 25.2 %all-gather.15.cloned.1.call-done = bf16[2,1024,256]{2,1,0:T(8,128)(2,1)} async-done(((bf16[2,128,256]{2,1,0:T(8,128)(2,1)}), bf16[2,1024,256]{2,1,0:T(8,128)(2,1)}) %all-gather.15.cloned.1.call-update) | async-done | bytes 1048592 | tf_op jit(solution)/shard_map/all_gather | solution.py:100
  46.8 3.3 fusion
  50.7 51.7 %all-gather.25.cloned.1.call-done = bf16[16384,256]{0,1:T(8,128)(2,1)} async-done(((bf16[2048,256]{0,1:T(8,128)(2,1)}), bf16[16384,256]{0,1:T(8,128)(2,1)}) %all-gather.25.cloned.1.call-update) | async-done | bytes 8388624 | tf_op jit(solution)/shard_map/all_gather | solution.py:116
  102.4 16.2 %copy.73 = bf16[32,8,8,2048]{3,2,1,0:T(8,128)(2,1)} copy(bf16[32,8,8,2048]{3,1,2,0:T(8,128)(2,1)} %bitcast.96) | data formatting | bytes 16777216
  118.6 10.4 %bitcast_reduce_fusion = bf16[2048,256]{0,1:T(8,128)(2,1)S(1)} fusion(bf16[32,8,8,2048]{3,2,1,0:T(8,128)(2,1)} %copy.73), kind=kLoop, calls=%fused_computation.5 | loop fusion | flops 3670016 | bytes 9437184 | tf_op jit(solution)/shard_map/reduce_sum | solution.py:115
  132.7 2.8 collective-permute-start.5
  142.1 2.7 collective-permute-start.3
  145.0 2.9 collective-permute-done.3
  148.0 18.6 %all-gather.17.cloned.1.call-done = bf16[2,1024,256]{1,2,0:T(8,128)(2,1)} async-done(((bf16[2,128,256]{1,2,0:T(8,128)(2,1)}), bf16[2,1024,256]{1,2,0:T(8,128)(2,1)}) %all-gather.17.cloned.1.call-update) | async-done | bytes 1048592 | tf_op jit(solution)/shard_map/all_gather | solution.py:100
  172.2 2.9 fusion.6
  175.4 35.5 %all-gather.27.cloned.1.call-done = bf16[8192,256]{0,1:T(8,128)(2,1)} async-done(((bf16[1024,256]{0,1:T(8,128)(2,1)}), bf16[8192,256]{0,1:T(8,128)(2,1)}) %all-gather.27.cloned.1.call-update) | async-done | bytes 4194320 | tf_op jit(solution)/shard_map/all_gather | solution.py:116
  210.8 6.5 copy.74
  217.4 3.5 bitcast_reduce_fusion.1
  226.0 2.7 collective-permute-start.10
  238.7 2.8 collective-permute-start.7
  246.0 2.6 collective-permute-done.8
  248.7 16.5 %all-gather.19.cloned.1.call-done = bf16[2,1024,256]{1,2,0:T(8,128)(2,1)} async-done(((bf16[2,128,256]{1,2,0:T(8,128)(2,1)}), bf16[2,1024,256]{1,2,0:T(8,128)(2,1)}) %all-gather.19.cloned.1.call-update) | async-done | bytes 1048592 | tf_op jit(solution)/shard_map/all_gather | solution.py:100
  273.3 28.9 %all-gather.29.cloned.1.call-done = bf16[4096,256]{0,1:T(8,128)(2,1)} async-done(((bf16[512,256]{0,1:T(8,128)(2,1)}), bf16[4096,256]{0,1:T(8,128)(2,1)}) %all-gather.29.cloned.1.call-update) | async-done | bytes 2097168 | tf_op jit(solution)/shard_map/all_gather | solution.py:116
  302.2 2.5 copy.75
  311.3 2.8 collective-permute-start.17
  328.6 2.8 collective-permute-start.13
  337.1 2.8 collective-permute-start.15
  340.1 3.7 collective-permute-done.15
  343.8 13.7 %all-gather.21.cloned.1.call-done = bf16[2,1024,256]{1,2,0:T(8,128)(2,1)} async-done(((bf16[2,128,256]{1,2,0:T(8,128)(2,1)}), bf16[2,1024,256]{1,2,0:T(8,128)(2,1)}) %all-gather.21.cloned.1.call-update) | async-done | bytes 1048592 | tf_op jit(solution)/shard_map/all_gather | solution.py:100
  365.6 26.7 %all-gather.31.cloned.1.call-done = bf16[2048,256]{0,1:T(8,128)(2,1)} async-done(((bf16[256,256]{0,1:T(8,128)(2,1)}), bf16[2048,256]{0,1:T(8,128)(2,1)}) %all-gather.31.cloned.1.call-update) | async-done | bytes 1048592 | tf_op jit(solution)/shard_map/all_gather | solution.py:116
  398.9 2.8 collective-permute-start.26
  413.4 6.2 collective-permute-start.29
  425.1 2.8 collective-permute-start.21
  437.7 5.3 collective-permute-start.24
  443.1 3.3 collective-permute-done.24
  447.1 7.8 all-gather.23.cloned.1.call-done
  460.9 18.3 %all-gather.4 = bf16[1024,256]{0,1:T(8,128)(2,1)S(1)} all-gather(bf16[128,256]{0,1:T(8,128)(2,1)S(1)} %fusion.14), channel_id=6, replica_groups=mesh['leaf'=32,'front'=8] {'front'}, dimensions={0}, use_global_device_ids=true | all-gather | bytes 589824 | tf_op jit(solution)/shard_map/all_gather | solution.py:116
  482.0 6.7 collective-permute-done.30
  488.8 2.7 collective-permute-start.31
  491.4 5.8 collective-permute-done.31
  497.4 6.0 collective-permute-done.32
  504.8 13.7 %collective-permute-done.33 = bf16[512,256]{0,1:T(8,128)(2,1)S(1)} collective-permute-done((bf16[512,256]{0,1:T(8,128)(2,1)S(1)}, bf16[512,256]{0,1:T(8,128)(2,1)S(1)}, u32[]{:S(2)}, u32[]{:S(2)}) %collective-permute-start.33) | collective-permute-done | bytes 262176 | tf_op jit(solution)/shard_map/ppermute | solution.py:18
  518.6 4.6 collective-permute-start.34
  523.2 12.4 %collective-permute-done.34 = bf16[512,256]{0,1:T(8,128)(2,1)S(1)} collective-permute-done((bf16[512,256]{0,1:T(8,128)(2,1)S(1)}, bf16[512,256]{0,1:T(8,128)(2,1)S(1)}, u32[]{:S(2)}, u32[]{:S(2)}) %collective-permute-start.34) | collective-permute-done | bytes 262176 | tf_op jit(solution)/shard_map/ppermute | solution.py:18
  539.3 13.7 %all_to_all.25 = bf16[8,128,256]{2,1,0:T(8,128)(2,1)S(1)} all-to-all(bf16[8,128,256]{2,1,0:T(8,128)(2,1)S(1)} %copy.50), channel_id=1, replica_groups=mesh['leaf'=32,'front'=8] {'front'}, dimensions={0} | all-to-all | bytes 1048576 | tf_op jit(solution)/shard_map/all_to_all | solution.py:172
  554.0 59.7 %all-reduce.6.cloned.1.call-done = bf16[256,256]{0,1:T(8,128)(2,1)} async-done(((bf16[256,256]{0,1:T(8,128)(2,1)}), bf16[256,256]{0,1:T(8,128)(2,1)}) %all-reduce.6.cloned.1.call-update) | async-done | bytes 131088 | tf_op jit(solution)/shard_map/psum | solution.py:142
  616.2 4.1 collective-permute-done.35
  620.4 2.7 collective-permute-start.36
  623.1 5.4 collective-permute-done.36
  630.0 3.9 collective-permute-done.37
  637.2 6.9 collective-permute-done.38
  648.9 24.9 %all_to_all.26 = bf16[8,128,256]{2,1,0:T(8,128)(2,1)S(1)} all-to-all(bf16[8,128,256]{2,1,0:T(8,128)(2,1)S(1)} %copy.54), channel_id=1, replica_groups=mesh['leaf'=32,'front'=8] {'front'}, dimensions={0} | all-to-all | bytes 1048576 | tf_op jit(solution)/shard_map/all_to_all | solution.py:172
  674.9 62.8 %all-reduce.8.cloned.1.call-done = bf16[512,256]{0,1:T(8,128)(2,1)} async-done(((bf16[512,256]{0,1:T(8,128)(2,1)}), bf16[512,256]{0,1:T(8,128)(2,1)}) %all-reduce.8.cloned.1.call-update) | async-done | bytes 262160 | tf_op jit(solution)/shard_map/psum | solution.py:142
  740.3 4.1 collective-permute-done.39
  744.5 2.8 collective-permute-start.40
  747.2 5.4 collective-permute-done.40
  755.5 4.1 collective-permute-done.41
  764.4 20.9 %all_to_all.27 = bf16[8,128,256]{2,1,0:T(8,128)(2,1)S(1)} all-to-all(bf16[8,128,256]{2,1,0:T(8,128)(2,1)S(1)} %copy.58), channel_id=1, replica_groups=mesh['leaf'=32,'front'=8] {'front'}, dimensions={0} | all-to-all | bytes 1048576 | tf_op jit(solution)/shard_map/all_to_all | solution.py:172
  786.5 63.8 %all-reduce.10.cloned.1.call-done = bf16[1024,256]{0,1:T(8,128)(2,1)} async-done(((bf16[1024,256]{0,1:T(8,128)(2,1)}), bf16[1024,256]{0,1:T(8,128)(2,1)}) %all-reduce.10.cloned.1.call-update) | async-done | bytes 524304 | tf_op jit(solution)/shard_map/psum | solution.py:142
  853.5 4.0 collective-permute-done.42
  858.3 3.0 collective-permute-start.43
  861.3 4.4 collective-permute-done.43
  869.4 20.0 %all_to_all.28 = bf16[8,128,256]{2,1,0:T(8,128)(2,1)S(1)} all-to-all(bf16[8,128,256]{2,1,0:T(8,128)(2,1)S(1)} %copy.62), channel_id=1, replica_groups=mesh['leaf'=32,'front'=8] {'front'}, dimensions={0} | all-to-all | bytes 1048576 | tf_op jit(solution)/shard_map/all_to_all | solution.py:172
  890.9 65.6 %all-reduce.12.cloned.1.call-done = bf16[2048,256]{0,1:T(8,128)(2,1)} async-done(((bf16[2048,256]{0,1:T(8,128)(2,1)}), bf16[2048,256]{0,1:T(8,128)(2,1)}) %all-reduce.12.cloned.1.call-update) | async-done | bytes 1048592 | tf_op jit(solution)/shard_map/psum | solution.py:142
  956.6 2.6 fusion.133
  961.6 2.9 collective-permute-done.44
  966.5 8.3 all-to-all-start.4
  978.9 5.2 all-to-all-done.4
  (305 shorter events, 183.6 us)
Async XLA Ops:
  7.2 36.2 %all-gather.15.cloned.1.call-start = ((), (), s32[]{:S(2)}) async-start(), calls=%async_computation.5 | async-start | bytes 1179648 | tf_op jit(solution)/shard_map/all_gather | solution.py:100
  7.2 4.1 collective-permute-start.1
  12.8 89.6 %all-gather.25.cloned.1.call-start = ((), (), s32[]{:S(2)}) async-start(), calls=%async_computation.14 | async-start | bytes 9437184 | tf_op jit(solution)/shard_map/all_gather | solution.py:116
  13.8 4.3 collective-permute-start
  50.2 116.4 %all-gather.17.cloned.1.call-start = ((), (), s32[]{:S(2)}) async-start(), calls=%async_computation.6 | async-start | bytes 1179648 | tf_op jit(solution)/shard_map/all_gather | solution.py:100
  129.5 3.2 collective-permute-start.4
  132.7 4.7 collective-permute-start.5
  138.1 72.7 %all-gather.27.cloned.1.call-start = ((), (), s32[]{:S(2)}) async-start(), calls=%async_computation.15 | async-start | bytes 4718592 | tf_op jit(solution)/shard_map/all_gather | solution.py:116
  138.2 3.2 collective-permute-start.2
  142.1 5.8 collective-permute-start.3
  175.1 90.0 %all-gather.19.cloned.1.call-start = ((), (), s32[]{:S(2)}) async-start(), calls=%async_computation.7 | async-start | bytes 1179648 | tf_op jit(solution)/shard_map/all_gather | solution.py:100
  222.2 3.2 collective-permute-start.9
  226.0 4.9 collective-permute-start.10
  231.8 3.2 collective-permute-start.11
  235.7 66.5 %all-gather.29.cloned.1.call-start = ((), (), s32[]{:S(2)}) async-start(), calls=%async_computation.16 | async-start | bytes 2359296 | tf_op jit(solution)/shard_map/all_gather | solution.py:116
  235.8 2.9 collective-permute-start.6
  238.7 4.7 collective-permute-start.7
  244.1 4.5 collective-permute-start.8
  273.2 84.3 %all-gather.21.cloned.1.call-start = ((), (), s32[]{:S(2)}) async-start(), calls=%async_computation.8 | async-start | bytes 1179648 | tf_op jit(solution)/shard_map/all_gather | solution.py:100
  308.1 3.2 collective-permute-start.16
  311.3 4.7 collective-permute-start.17
  316.7 3.4 collective-permute-start.18
  321.1 4.1 collective-permute-start.19
  325.8 66.5 %all-gather.31.cloned.1.call-start = ((), (), s32[]{:S(2)}) async-start(), calls=%async_computation.17 | async-start | bytes 1179648 | tf_op jit(solution)/shard_map/all_gather | solution.py:116
  325.9 2.7 collective-permute-start.12
  328.6 4.4 collective-permute-start.13
  333.0 3.4 collective-permute-start.14
  337.1 6.7 collective-permute-start.15
  363.1 61.9 %slice-start.4 = ((f32[496,256]{1,0:T(8,128)}), f32[16,256]{1,0:T(8,128)S(1)}, s32[]{:S(2)}) async-start(f32[496,256]{1,0:T(8,128)} %param.6), calls=%async_computation.22 | async-start | bytes 32768 | tf_op jit(solution)/shard_map/slice | solution.py:112
  365.4 89.5 %all-gather.23.cloned.1.call-start = ((), (), s32[]{:S(2)}) async-start(), calls=%async_computation.9 | async-start | bytes 1179648 | tf_op jit(solution)/shard_map/all_gather | solution.py:100
  395.7 3.2 collective-permute-start.25
  398.9 4.7 collective-permute-start.26
  403.6 3.2 collective-permute-start.27
  408.1 4.3 collective-permute-start.28
  413.4 8.0 collective-permute-start.29
  422.1 191.7 %all-reduce.6.cloned.1.call-start = ((), (), s32[]{:S(2)}) async-start(), calls=%async_computation.10 | async-start | bytes 262144 | tf_op jit(solution)/shard_map/psum | solution.py:142
  422.2 2.9 collective-permute-start.20
  425.1 4.2 collective-permute-start.21
  429.3 2.9 collective-permute-start.22
  432.1 4.8 collective-permute-start.23
  437.7 8.7 collective-permute-start.24
  480.9 7.8 collective-permute-start.30
  488.8 8.4 collective-permute-start.31
  497.3 6.1 collective-permute-start.32
  503.5 15.0 %collective-permute-start.33 = (bf16[512,256]{0,1:T(8,128)(2,1)S(1)}, bf16[512,256]{0,1:T(8,128)(2,1)S(1)}, u32[]{:S(2)}, u32[]{:S(2)}) collective-permute-start(bf16[512,256]{0,1:T(8,128)(2,1)S(1)} %fusion.32), channel_id=1, source_target_pairs={{0,64},{64,0},{8,72},{72,8},{16,80},{80,16},{24,88},{88,24},{32,96... | collective-permute-start | bytes 786440 | tf_op jit(solution)/shard_map/ppermute | solution.py:18
  518.6 17.0 %collective-permute-start.34 = (bf16[512,256]{0,1:T(8,128)(2,1)S(1)}, bf16[512,256]{0,1:T(8,128)(2,1)S(1)}, u32[]{:S(2)}, u32[]{:S(2)}) collective-permute-start(bf16[512,256]{0,1:T(8,128)(2,1)S(1)} %fusion.51), channel_id=1, source_target_pairs={{0,128},{128,0},{8,136},{136,8},{16,144},{144,16},{24,152},{152,24... | collective-permute-start | bytes 786440 | tf_op jit(solution)/shard_map/ppermute | solution.py:18
  554.0 183.7 %all-reduce.8.cloned.1.call-start = ((), (), s32[]{:S(2)}) async-start(), calls=%async_computation.11 | async-start | bytes 524288 | tf_op jit(solution)/shard_map/psum | solution.py:142
  615.0 5.3 collective-permute-start.35
  620.4 8.2 collective-permute-start.36
  628.6 5.3 collective-permute-start.37
  634.8 9.2 collective-permute-start.38
  646.1 91.5 %copy-start.4 = (bf16[512,256]{0,1:T(8,128)(2,1)S(1)}, bf16[512,256]{0,1:T(8,128)(2,1)}, u32[]{:S(2)}) copy-start(bf16[512,256]{0,1:T(8,128)(2,1)} %copy-done.3) | copy-start | bytes 786436
  674.8 89.1 %copy-start.18 = (s32[8]{0:T(128)S(1)}, s32[8]{0:T(128)}, u32[]{:S(2)}) copy-start(s32[8]{0:T(128)} %get-tuple-element.54) | copy-start | bytes 100
  674.8 175.5 %all-reduce.10.cloned.1.call-start = ((), (), s32[]{:S(2)}) async-start(), calls=%async_computation.12 | async-start | bytes 1048576 | tf_op jit(solution)/shard_map/psum | solution.py:142
  739.1 5.3 collective-permute-start.39
  744.5 8.2 collective-permute-start.40
  754.1 5.5 collective-permute-start.41
  786.5 82.4 %copy-start.17 = (s32[8]{0:T(128)S(1)}, s32[8]{0:T(128)}, u32[]{:S(2)}) copy-start(s32[8]{0:T(128)} %get-tuple-element.57) | copy-start | bytes 100
  786.5 170.1 %all-reduce.12.cloned.1.call-start = ((), (), s32[]{:S(2)}) async-start(), calls=%async_computation.13 | async-start | bytes 2097152 | tf_op jit(solution)/shard_map/psum | solution.py:142
  852.2 5.3 collective-permute-start.42
  858.3 7.5 collective-permute-start.43
  890.9 74.3 %copy-start.16 = (s32[8]{0:T(128)S(1)}, s32[8]{0:T(128)}, u32[]{:S(2)}) copy-start(s32[8]{0:T(128)} %get-tuple-element.60) | copy-start | bytes 100
  959.2 5.3 collective-permute-start.44
  966.5 17.6 %all-to-all-start.4 = ((bf16[8,128,256]{2,1,0:T(8,128)(2,1)}), bf16[8,128,256]{2,1,0:T(8,128)(2,1)S(1)}, u32[]{:S(2)}, u32[]{:S(2)}) async-start(bf16[8,128,256]{2,1,0:T(8,128)(2,1)} %copy.66), calls=%async_computation.4 | async-start | bytes 1048576 | tf_op jit(solution)/shard_map/all_to_all | solution.py:172
  (21 other events, 430.5 us)
Sparse Core Ops, SparseCore 0:
  12.9 30.4 all-gather.14
  50.3 52.0 all-gather.24
  138.2 28.2 all-gather.16
  175.2 35.5 all-gather.26
  235.8 29.2 all-gather.18
  273.3 28.7 all-gather.28
  326.0 31.4 all-gather.20
  365.5 26.7 all-gather.30
  422.2 32.6 all-gather.22
  554.1 59.6 all-reduce.5
  674.9 62.6 all-reduce.7
  786.6 63.7 all-reduce.9
  891.1 65.4 all-reduce.11
